TPU v7x, 256 devices: a whole 4x4x8 slice. The times are simulated.
256 devices in a mesh: gx: 4 (over x_lo, core), gy: 8 (over z), gz: 8 (over x_hi, y).
Axes of the slice: x: 4 (x_hi: 2, x_lo: 2; x = x_hi * 2 + x_lo), y: 4, z: 8, core: 2. Of those that a mesh axis runs over, the one named last changes fastest.
Arguments:
- traces: bfloat16 [2, 4, 8, 8, 512, 768], P(None, 'gx', 'gy', 'gz'), may hold values from -6 to 6
- sources: bfloat16 [2, 4, 8, 8, 512, 768], P(None, 'gx', 'gy', 'gz'), may hold values from -4 to 4
- local_ops: bfloat16 [2, 4, 8, 8, 768, 768], P(None, 'gx', 'gy', 'gz'), may hold values from -0.15625 to 0.15625
- plane_coupling: bfloat16 [4, 64, 64], P('gx'), may hold values from -0.375 to 0.375
- face_owner: int32 [4, 64], P('gx'), may hold values from 0 to 63, each once within a row
Outputs:
- new_traces: bfloat16 [2, 4, 8, 8, 512, 768], P(None, 'gx', 'gy', 'gz')
Inputs may be any that keep to these rules, and one draw needn't show every extreme that they name: `face_owner`: each row is a permutation of the 64 plane positions.
All inputs are finite; a program needn't handle non-finite values.
Results may differ from a plain program's by a relative error of at most 0.0062.
Values may be sent and summed in bfloat16 or wider, within the bound.
A program may use at most 64 MiB of HBM per device.

v0:
```python
import jax
import jax.numpy as jnp
from jax import lax
from jax.sharding import PartitionSpec as P

SWEEPS = 2


def with_halo(block, sides, width):
    for axis, dim in sides:
        count = lax.axis_size(axis)
        forward = [(i, i + 1) for i in range(count - 1)]
        forward.append((count - 1, 0))
        backward = [(target, source) for source, target in forward]
        low = lax.ppermute(
            lax.slice_in_dim(block, block.shape[dim] - width, None, axis=dim), axis, forward
        )
        high = lax.ppermute(lax.slice_in_dim(block, 0, width, axis=dim), axis, backward)
        block = jnp.concatenate([low, block, high], axis=dim)
    return block


def on_device(traces, sources, local_ops, plane_coupling, face_owner):
    columns_all = local_ops.shape[-1]
    slab_width = columns_all // 6
    slab_rows = traces.shape[4]
    count_y = lax.axis_size("gy")
    count_z = lax.axis_size("gz")
    plane_size = count_y * count_z
    block_rows_count = slab_rows // plane_size
    operators = local_ops.reshape(2, columns_all, columns_all)
    source_rows = sources.reshape(2, slab_rows, columns_all).astype(jnp.float32)
    incoming = traces.reshape(2, slab_rows, columns_all)
    owners = face_owner.reshape(plane_size)
    select = (owners[:, None] == jnp.arange(plane_size, dtype=jnp.int32)[None, :]).astype(
        jnp.float32
    )
    mixing = jnp.dot(
        plane_coupling.reshape(plane_size, plane_size).astype(jnp.float32),
        select,
        precision=lax.Precision.HIGHEST,
    ).astype(jnp.bfloat16)
    for sweep_step in range(SWEEPS):
        real_part = (
            jnp.dot(incoming[0], operators[0], preferred_element_type=jnp.float32)
            - jnp.dot(incoming[1], operators[1], preferred_element_type=jnp.float32)
            + source_rows[0]
        )
        imag_part = (
            jnp.dot(incoming[0], operators[1], preferred_element_type=jnp.float32)
            + jnp.dot(incoming[1], operators[0], preferred_element_type=jnp.float32)
            + source_rows[1]
        )
        outgoing = (
            jnp.stack([real_part, imag_part])
            .astype(jnp.bfloat16)
            .reshape(2, slab_rows, 6, slab_width)
        )
        along_x = with_halo(outgoing[:, :, 0:2, :], (("gx", 2),), 1)
        partial_faces = jnp.concatenate(
            [along_x[:, :, 0:1], along_x[:, :, 3:4], outgoing[:, :, 2:6]], axis=2
        )
        blocks = partial_faces.reshape(2, plane_size, block_rows_count, 6, slab_width)
        update_block_rows = lax.all_to_all(
            blocks, ("gy", "gz"), split_axis=1, concat_axis=1, tiled=True
        )
        row_count = update_block_rows.shape[2]
        grid_view = update_block_rows.reshape(2, count_y, count_z, row_count, 6, slab_width)
        moved = jnp.stack(
            [
                grid_view[:, :, :, :, 0],
                grid_view[:, :, :, :, 1],
                jnp.roll(grid_view[:, :, :, :, 3], 1, axis=1),
                jnp.roll(grid_view[:, :, :, :, 2], -1, axis=1),
                jnp.roll(grid_view[:, :, :, :, 5], 1, axis=2),
                jnp.roll(grid_view[:, :, :, :, 4], -1, axis=2),
            ],
            axis=4,
        )
        block_rows = moved.reshape(2, plane_size, row_count * columns_all)
        coupled = jnp.einsum("pq,rqc->rpc", mixing, block_rows, preferred_element_type=jnp.float32)
        updated = (block_rows.astype(jnp.float32) - coupled).astype(jnp.bfloat16)
        updated = updated.reshape(2, plane_size, row_count, 6, slab_width)
        returned = lax.all_to_all(updated, ("gy", "gz"), split_axis=1, concat_axis=1, tiled=True)
        incoming = returned.reshape(2, slab_rows, columns_all)
    return incoming.reshape(traces.shape)


def solution(mesh):
    placed = (
        P(None, "gx", "gy", "gz", None, None),
        P(None, "gx", "gy", "gz", None, None),
        P(None, "gx", "gy", "gz", None, None),
        P("gx", None, None),
        P("gx", None),
    )
    return jax.shard_map(
        on_device,
        mesh=mesh,
        in_specs=placed,
        out_specs=P(None, "gx", "gy", "gz", None, None),
        check_vma=False,
    )
```

profile of v0, /device:TPU:8, one launch (start us, length us, event | category | flops | bytes accessed | tf_op | source)
XLA Modules:
  0.0 268.1 jit_solution(3088411182501243371)
XLA Ops:
  0.0 2.4 fusion.15
  2.5 2.0 fusion.22
  7.6 1.7 add_convert_fusion.3
  9.4 2.3 copy.56
  11.7 2.3 copy.57
  15.3 1.7 collective-permute-start.1
  17.1 5.1 %collective-permute-done = bf16[2,512,1,128]{1,3,2,0:T(8,128)(2,1)S(1)} collective-permute-done((bf16[2,512,1,128]{1,3,2,0:T(8,128)(2,1)S(1)}, bf16[2,512,1,128]{1,3,2,0:T(8,128)(2,1)S(1)}, u32[]{:S(2)}, u32[]{:S(2)}) %collective-permute-start) | collective-permute-done | bytes 262176 | tf_op jit(solution)/shard_map/ppermute | solution.py:15
  24.3 2.6 copy.58
  26.9 2.8 %copy.59 = bf16[2,64,8,6,128]{4,2,3,0,1:T(8,128)(2,1)} copy(bf16[2,64,8,6,128]{4,2,1,3,0:T(8,128)(2,1)} %bitcast.168) | data formatting | bytes 3145728 | tf_op jit(solution)/shard_map/reshape | solution.py:63
  29.7 14.6 %all-to-all-start = ((bf16[2,64,8,6,128]{4,2,3,0,1:T(8,128)(2,1)}), bf16[2,64,8,6,128]{4,2,3,0,1:T(8,128)(2,1)}, u32[]{:S(2)}, u32[]{:S(2)}) async-start(bf16[2,64,8,6,128]{4,2,3,0,1:T(8,128)(2,1)} %copy.59), calls=%async_computation | async-start | bytes 3145728 | tf_op jit(solution)/shard_map/all_to_all | solution.py:64
  44.5 40.1 %all-to-all-done = bf16[2,64,8,6,128]{4,2,3,0,1:T(8,128)(2,1)} async-done(((bf16[2,64,8,6,128]{4,2,3,0,1:T(8,128)(2,1)}), bf16[2,64,8,6,128]{4,2,3,0,1:T(8,128)(2,1)}, u32[]{:S(2)}, u32[]{:S(2)}) %all-to-all-start) | async-done | bytes 1572896 | tf_op jit(solution)/shard_map/all_to_all | solution.py:64
  87.4 1.8 fusion.3
  89.2 4.5 %reshape.67 = bf16[2,64,8,6,128]{4,3,2,1,0:T(8,128)(2,1)} reshape(bf16[2,64,6144]{2,1,0:T(8,128)(2,1)} %fusion.3) | data formatting | bytes 3145728 | tf_op jit(solution)/shard_map/reshape | solution.py:83
  93.7 1.9 copy.67
  95.6 48.0 %all_to_all.20 = bf16[2,64,8,6,128]{4,2,3,0,1:T(8,128)(2,1)S(1)} all-to-all(bf16[2,64,8,6,128]{4,2,3,0,1:T(8,128)(2,1)S(1)} %copy.67), channel_id=1, replica_groups=mesh['gx'=4,'gy'=8,'gz'=8] {'gy','gz'}, dimensions={1} | all-to-all | bytes 3145728 | tf_op jit(solution)/shard_map/all_to_all | solution.py:84
  144.7 1.7 add_convert_fusion
  146.5 2.3 copy.71
  148.8 2.4 fusion.19
  151.2 2.9 %add_convert_fusion.1 = bf16[512,768]{1,0:T(8,128)(2,1)} fusion(f32[512,768]{1,0:T(8,128)S(1)} %fusion.19, f32[2,1,1,1,512,768]{5,4,3,2,1,0:T(8,128)S(1)} %convert_element_type.26, bf16[2,1,1,1,768,768]{5,4,3,2,1,0:T(8,128)(2,1)S(1)} %copy-done.3, bf16[2,64,8,6,128]{4,2,3,0,1:T(8,128)(2,1)} %copy-done.7), kind=kOutput, calls=%fused_computation.19 | convolution fusion | flops 605159424 | bytes 5898240 | tf_op jit(solution)/shard_map/dot_general | solution.py:46
  157.5 6.0 %collective-permute-done.2 = bf16[2,512,1,128]{1,3,2,0:T(8,128)(2,1)S(1)} collective-permute-done((bf16[2,512,1,128]{1,3,2,0:T(8,128)(2,1)S(1)}, bf16[2,512,1,128]{1,3,2,0:T(8,128)(2,1)S(1)}, u32[]{:S(2)}, u32[]{:S(2)}) %collective-permute-start.2) | collective-permute-done | bytes 262176 | tf_op jit(solution)/shard_map/ppermute | solution.py:15
  164.8 47.6 %all_to_all.21 = bf16[2,64,8,6,128]{4,2,3,0,1:T(8,128)(2,1)S(1)} all-to-all(bf16[2,64,8,6,128]{4,2,3,0,1:T(8,128)(2,1)S(1)} %copy.73), channel_id=1, replica_groups=mesh['gx'=4,'gy'=8,'gz'=8] {'gy','gz'}, dimensions={1} | all-to-all | bytes 3145728 | tf_op jit(solution)/shard_map/all_to_all | solution.py:64
  213.8 1.8 fusion.2
  215.5 3.6 %reshape.71 = bf16[2,64,8,6,128]{4,3,2,1,0:T(8,128)(2,1)S(1)} reshape(bf16[2,64,6144]{2,1,0:T(8,128)(2,1)} %fusion.2) | data formatting | bytes 3145728 | tf_op jit(solution)/shard_map/reshape | solution.py:83
  219.4 47.4 %all_to_all.22 = bf16[2,64,8,6,128]{4,2,3,0,1:T(8,128)(2,1)S(1)} all-to-all(bf16[2,64,8,6,128]{4,2,3,0,1:T(8,128)(2,1)S(1)} %copy.81), channel_id=1, replica_groups=mesh['gx'=4,'gy'=8,'gz'=8] {'gy','gz'}, dimensions={1} | all-to-all | bytes 3145728 | tf_op jit(solution)/shard_map/all_to_all | solution.py:84
  (72 shorter events, 18.0 us)
Async XLA Ops:
  0.0 44.3 %copy-start = (bf16[1,64,64]{2,1,0:T(8,128)(2,1)S(1)}, bf16[1,64,64]{2,1,0:T(8,128)(2,1)}, u32[]{:S(2)}) copy-start(bf16[1,64,64]{2,1,0:T(8,128)(2,1)} %param.8) | copy-start | bytes 24580
  0.0 2.4 copy-start.1
  2.5 2.0 copy-start.8
  4.5 1.4 copy-start.9
  14.0 9.0 %copy-start.5 = (bf16[512,768]{0,1:T(8,128)(2,1)S(1)}, bf16[512,768]{0,1:T(8,128)(2,1)}, u32[]{:S(2)}) copy-start(bf16[512,768]{0,1:T(8,128)(2,1)} %copy.56) | copy-start | bytes 2359300
  14.0 9.0 %copy-start.6 = (bf16[512,768]{0,1:T(8,128)(2,1)S(1)}, bf16[512,768]{0,1:T(8,128)(2,1)}, u32[]{:S(2)}) copy-start(bf16[512,768]{0,1:T(8,128)(2,1)} %copy.57) | copy-start | bytes 2359300
  15.3 6.9 %collective-permute-start = (bf16[2,512,1,128]{1,3,2,0:T(8,128)(2,1)S(1)}, bf16[2,512,1,128]{1,3,2,0:T(8,128)(2,1)S(1)}, u32[]{:S(2)}, u32[]{:S(2)}) collective-permute-start(bf16[2,512,1,128]{1,3,2,0:T(8,128)(2,1)S(1)} %get-tuple-element.15), channel_id=1, source_target_pairs={{0,64},{64,128},{128,192},{192,0},{1,65},{65,129},{129,193},{193,1... | collective-permute-start | bytes 786440 | tf_op jit(solution)/shard_map/ppermute | solution.py:15
  15.3 7.6 %collective-permute-start.1 = (bf16[2,512,1,128]{1,3,2,0:T(8,128)(2,1)S(1)}, bf16[2,512,1,128]{1,3,2,0:T(8,128)(2,1)S(1)}, u32[]{:S(2)}, u32[]{:S(2)}) collective-permute-start(bf16[2,512,1,128]{1,3,2,0:T(8,128)(2,1)S(1)} %get-tuple-element.16), channel_id=1, source_target_pairs={{64,0},{128,64},{192,128},{0,192},{65,1},{129,65},{193,129},{1,193... | collective-permute-start | bytes 786440 | tf_op jit(solution)/shard_map/ppermute | solution.py:18
  29.7 14.6 %copy-start.10 = (s32[1,64]{1,0:T(1,128)S(1)}, s32[1,64]{1,0:T(1,128)}, u32[]{:S(2)}) copy-start(s32[1,64]{1,0:T(1,128)} %param.9) | copy-start | bytes 772
  29.7 54.9 %all-to-all-start = ((bf16[2,64,8,6,128]{4,2,3,0,1:T(8,128)(2,1)}), bf16[2,64,8,6,128]{4,2,3,0,1:T(8,128)(2,1)}, u32[]{:S(2)}, u32[]{:S(2)}) async-start(bf16[2,64,8,6,128]{4,2,3,0,1:T(8,128)(2,1)} %copy.59), calls=%async_computation | async-start | bytes 3145728 | tf_op jit(solution)/shard_map/all_to_all | solution.py:64
  95.6 48.0 %copy-start.2 = (bf16[2,1,1,1,768,768]{5,4,3,2,1,0:T(8,128)(2,1)S(1)}, bf16[2,1,1,1,768,768]{5,4,3,2,1,0:T(8,128)(2,1)}, u32[]{:S(2)}) copy-start(bf16[2,1,1,1,768,768]{5,4,3,2,1,0:T(8,128)(2,1)} %param.7) | copy-start | bytes 7077892
  143.6 1.1 copy-start.7
  148.8 2.5 copy-start.3
  154.1 1.5 copy-start.4
  155.7 7.8 %collective-permute-start.2 = (bf16[2,512,1,128]{1,3,2,0:T(8,128)(2,1)S(1)}, bf16[2,512,1,128]{1,3,2,0:T(8,128)(2,1)S(1)}, u32[]{:S(2)}, u32[]{:S(2)}) collective-permute-start(bf16[2,512,1,128]{1,3,2,0:T(8,128)(2,1)S(1)} %get-tuple-element.9), channel_id=1, source_target_pairs={{0,64},{64,128},{128,192},{192,0},{1,65},{65,129},{129,193},{193,1... | collective-permute-start | bytes 786440 | tf_op jit(solution)/shard_map/ppermute | solution.py:15
  155.7 7.7 %collective-permute-start.3 = (bf16[2,512,1,128]{1,3,2,0:T(8,128)(2,1)S(1)}, bf16[2,512,1,128]{1,3,2,0:T(8,128)(2,1)S(1)}, u32[]{:S(2)}, u32[]{:S(2)}) collective-permute-start(bf16[2,512,1,128]{1,3,2,0:T(8,128)(2,1)S(1)} %get-tuple-element.10), channel_id=1, source_target_pairs={{64,0},{128,64},{192,128},{0,192},{65,1},{129,65},{193,129},{1,193... | collective-permute-start | bytes 786440 | tf_op jit(solution)/shard_map/ppermute | solution.py:18
where the time goes:
time: 269 us; the launch traced here: 268 us
  blocking collectives  143 us (53%)
  waiting for transfers between devices  52 us (19%)
  local copies, waits for them, and re-layouts  31.3 us (12%)
  matrix products  19.5 us (7%)
  starting transfers between devices  18.2 us (7%)
  other arithmetic  3.57 us (1%)
    all_to_all x2, blocking collectives, on_device(): lax.all_to_all(updated, ('gy', 'gz'), split_axis=1, concat_axis=1, tiled=...  95.4 us
    all_to_all x1, blocking collectives, on_device(): lax.all_to_all(blocks, ('gy', 'gz'), split_axis=1, concat_axis=1, tiled=T...  47.6 us
    all_to_all x1, waiting for transfers between devices, on_device(): lax.all_to_all(blocks, ('gy', 'gz'), split_axis=1, concat_axis=1, tiled=T...  40.1 us
    all_to_all x1, starting transfers between devices, on_device(): lax.all_to_all(blocks, ('gy', 'gz'), split_axis=1, concat_axis=1, tiled=T...  14.6 us
    ppermute x2, waiting for transfers between devices, with_halo(): lax.ppermute(lax.slice_in_dim(block, block.shape[dim] - width, None, axis...  11.1 us
    reshape x4, local copies, waits for them, and re-layouts, on_device(): updated = updated.reshape(2, plane_size, row_count, 6, slab_width)  10.2 us
    another operation x4, local copies, waits for them, and re-layouts  8.4 us
  transfers between devices with their start and end apart: 5, of which 4 were waited for; matrix products, arithmetic and copies ran while one was open for 0% of the time, Pallas kernels for 0%

commit v1 on v0

--- a/solution.py
+++ b/solution.py
@@ -81,7 +81,15 @@
         coupled = jnp.einsum("pq,rqc->rpc", mixing, block_rows, preferred_element_type=jnp.float32)
         updated = (block_rows.astype(jnp.float32) - coupled).astype(jnp.bfloat16)
         updated = updated.reshape(2, plane_size, row_count, 6, slab_width)
-        returned = lax.all_to_all(updated, ("gy", "gz"), split_axis=1, concat_axis=1, tiled=True)
+        returned = jnp.concatenate(
+            lax.all_to_all(
+                jnp.stack(jnp.split(updated, lax.axis_size(("gy", "gz")), axis=1)),
+                ("gy", "gz"),
+                0,
+                0,
+            ),
+            axis=1,
+        )
         incoming = returned.reshape(2, slab_rows, columns_all)
     return incoming.reshape(traces.shape)
 

time: 269 us -> 325 us (1.21); the launches traced: 268 us -> 319 us
  local copies, waits for them, and re-layouts: 31.3 us -> 82.2 us
    unnamed x24 -> x150, local copies, waits for them, and re-layouts: 1.65 us -> 53.1 us
    reshape x4 -> x2, local copies, waits for them, and re-layouts: 10.2 us -> 8.09 us  [on_device(): updated = updated.reshape(2, plane_size, row_count, 6, slab_width)]
    another operation x4 -> x8, local copies, waits for them, and re-layouts: 8.4 us -> 9.87 us
where the time goes in v1:
time: 325 us; the launch traced here: 319 us
  blocking collectives  143 us (44%)
  local copies, waits for them, and re-layouts  82.2 us (25%)
  waiting for transfers between devices  52 us (16%)
  matrix products  19.8 us (6%)
  starting transfers between devices  18.2 us (6%)
  other arithmetic  3.57 us (1%)
    all_to_all x2, blocking collectives, on_device(): lax.all_to_all(jnp.stack(jnp.split(updated, lax.axis_size(('gy', 'gz')),...  95.3 us
    unnamed x150, local copies, waits for them, and re-layouts  53.1 us
    all_to_all x1, blocking collectives, on_device(): lax.all_to_all(blocks, ('gy', 'gz'), split_axis=1, concat_axis=1, tiled=T...  47.6 us
    all_to_all x1, waiting for transfers between devices, on_device(): lax.all_to_all(blocks, ('gy', 'gz'), split_axis=1, concat_axis=1, tiled=T...  40.1 us
    all_to_all x1, starting transfers between devices, on_device(): lax.all_to_all(blocks, ('gy', 'gz'), split_axis=1, concat_axis=1, tiled=T...  14.6 us
    ppermute x2, waiting for transfers between devices, with_halo(): lax.ppermute(lax.slice_in_dim(block, block.shape[dim] - width, None, axis...  11.1 us
    another operation x4, local copies, waits for them, and re-layouts  8.39 us
    reshape x2, local copies, waits for them, and re-layouts, on_device(): updated = updated.reshape(2, plane_size, row_count, 6, slab_width)  8.09 us
  transfers between devices with their start and end apart: 5, of which 4 were waited for; matrix products, arithmetic and copies ran while one was open for 0% of the time, Pallas kernels for 0%

profile of v1, /device:TPU:8, one launch (start us, length us, event | category | flops | bytes accessed | tf_op | source)
XLA Modules:
  0.0 319.4 jit_solution(12081410061274300644)
XLA Ops:
  0.0 2.4 fusion.15
  2.5 2.0 fusion.22
  7.6 1.7 add_convert_fusion.3
  9.4 2.3 copy.435
  11.7 2.3 copy.436
  15.3 1.7 collective-permute-start.1
  17.1 5.1 %collective-permute-done = bf16[2,512,1,128]{1,3,2,0:T(8,128)(2,1)S(1)} collective-permute-done((bf16[2,512,1,128]{1,3,2,0:T(8,128)(2,1)S(1)}, bf16[2,512,1,128]{1,3,2,0:T(8,128)(2,1)S(1)}, u32[]{:S(2)}, u32[]{:S(2)}) %collective-permute-start) | collective-permute-done | bytes 262176 | tf_op jit(solution)/shard_map/ppermute | solution.py:15
  24.3 2.6 copy.437
  26.9 2.8 copy.438
  29.7 14.6 %all-to-all-start = ((bf16[2,64,8,6,128]{4,2,3,0,1:T(8,128)(2,1)}), bf16[2,64,8,6,128]{4,2,3,0,1:T(8,128)(2,1)}, u32[]{:S(2)}, u32[]{:S(2)}) async-start(bf16[2,64,8,6,128]{4,2,3,0,1:T(8,128)(2,1)} %copy.438), calls=%async_computation | async-start | bytes 3145728 | tf_op jit(solution)/shard_map/all_to_all | solution.py:64
  44.5 40.1 %all-to-all-done = bf16[2,64,8,6,128]{4,2,3,0,1:T(8,128)(2,1)} async-done(((bf16[2,64,8,6,128]{4,2,3,0,1:T(8,128)(2,1)}), bf16[2,64,8,6,128]{4,2,3,0,1:T(8,128)(2,1)}, u32[]{:S(2)}, u32[]{:S(2)}) %all-to-all-start) | async-done | bytes 1572896 | tf_op jit(solution)/shard_map/all_to_all | solution.py:64
  87.4 1.8 fusion.3
  89.2 4.5 %reshape.72 = bf16[2,64,8,6,128]{4,3,2,1,0:T(8,128)(2,1)} reshape(bf16[2,64,6144]{2,1,0:T(8,128)(2,1)} %fusion.3) | data formatting | bytes 3145728 | tf_op jit(solution)/shard_map/reshape | solution.py:83
  143.8 47.9 %all_to_all.20 = bf16[64,2,1,8,6,128]{5,3,4,2,1,0:T(8,128)(2,1)S(1)} all-to-all(bf16[64,2,1,8,6,128]{5,3,4,2,1,0:T(8,128)(2,1)S(1)} %copy.509), channel_id=1, replica_groups=mesh['gx'=4,'gy'=8,'gz'=8] {'gy','gz'}, dimensions={0} | all-to-all | bytes 3145728 | tf_op jit(solution)/shard_map/all_to_all | solution.py:85
  191.8 2.1 copy-done.3
  194.7 1.9 fusion.19
  198.4 2.3 copy.512
  200.6 3.7 %add_convert_fusion.1 = bf16[512,768]{1,0:T(8,128)(2,1)} fusion(f32[512,768]{1,0:T(8,128)} %fusion.19, f32[2,1,1,1,512,768]{5,4,3,2,1,0:T(8,128)S(1)} %convert_element_type.26, bf16[2,1,1,1,768,768]{5,4,3,2,1,0:T(8,128)(2,1)} %param.7, bf16[2,64,1,8,6,128]{5,3,4,2,1,0:T(8,128)(2,1)} %bitcast.938), kind=kOutput, calls=%fused_computation.20 | convolution fusion | flops 605159424 | bytes 5898240 | tf_op jit(solution)/shard_map/dot_general | solution.py:46
  206.0 1.7 collective-permute-start.3
  207.7 6.0 %collective-permute-done.2 = bf16[2,512,1,128]{1,3,2,0:T(8,128)(2,1)S(1)} collective-permute-done((bf16[2,512,1,128]{1,3,2,0:T(8,128)(2,1)S(1)}, bf16[2,512,1,128]{1,3,2,0:T(8,128)(2,1)S(1)}, u32[]{:S(2)}, u32[]{:S(2)}) %collective-permute-start.2) | collective-permute-done | bytes 262176 | tf_op jit(solution)/shard_map/ppermute | solution.py:15
  215.0 47.6 %all_to_all.21 = bf16[2,64,8,6,128]{4,2,3,0,1:T(8,128)(2,1)S(1)} all-to-all(bf16[2,64,8,6,128]{4,2,3,0,1:T(8,128)(2,1)S(1)} %copy.514), channel_id=1, replica_groups=mesh['gx'=4,'gy'=8,'gz'=8] {'gy','gz'}, dimensions={1} | all-to-all | bytes 3145728 | tf_op jit(solution)/shard_map/all_to_all | solution.py:64
  264.0 1.8 fusion.2
  265.8 3.6 %reshape.77 = bf16[2,64,8,6,128]{4,3,2,1,0:T(8,128)(2,1)S(1)} reshape(bf16[2,64,6144]{2,1,0:T(8,128)(2,1)} %fusion.2) | data formatting | bytes 3145728 | tf_op jit(solution)/shard_map/reshape | solution.py:83
  270.7 47.4 %all_to_all.22 = bf16[64,2,1,8,6,128]{5,3,4,2,1,0:T(8,128)(2,1)S(1)} all-to-all(bf16[64,2,1,8,6,128]{5,3,4,2,1,0:T(8,128)(2,1)S(1)} %copy.585), channel_id=1, replica_groups=mesh['gx'=4,'gy'=8,'gz'=8] {'gy','gz'}, dimensions={0} | all-to-all | bytes 3145728 | tf_op jit(solution)/shard_map/all_to_all | solution.py:85
  (201 shorter events, 68.6 us)
Async XLA Ops:
  0.0 44.3 %copy-start = (bf16[1,64,64]{2,1,0:T(8,128)(2,1)S(1)}, bf16[1,64,64]{2,1,0:T(8,128)(2,1)}, u32[]{:S(2)}) copy-start(bf16[1,64,64]{2,1,0:T(8,128)(2,1)} %param.8) | copy-start | bytes 24580
  0.0 2.4 copy-start.2
  2.5 2.0 copy-start.8
  4.5 1.4 copy-start.9
  14.0 9.0 %copy-start.5 = (bf16[512,768]{0,1:T(8,128)(2,1)S(1)}, bf16[512,768]{0,1:T(8,128)(2,1)}, u32[]{:S(2)}) copy-start(bf16[512,768]{0,1:T(8,128)(2,1)} %copy.435) | copy-start | bytes 2359300
  14.0 9.0 %copy-start.6 = (bf16[512,768]{0,1:T(8,128)(2,1)S(1)}, bf16[512,768]{0,1:T(8,128)(2,1)}, u32[]{:S(2)}) copy-start(bf16[512,768]{0,1:T(8,128)(2,1)} %copy.436) | copy-start | bytes 2359300
  15.3 6.9 %collective-permute-start = (bf16[2,512,1,128]{1,3,2,0:T(8,128)(2,1)S(1)}, bf16[2,512,1,128]{1,3,2,0:T(8,128)(2,1)S(1)}, u32[]{:S(2)}, u32[]{:S(2)}) collective-permute-start(bf16[2,512,1,128]{1,3,2,0:T(8,128)(2,1)S(1)} %get-tuple-element.15), channel_id=1, source_target_pairs={{0,64},{64,128},{128,192},{192,0},{1,65},{65,129},{129,193},{193,1... | collective-permute-start | bytes 786440 | tf_op jit(solution)/shard_map/ppermute | solution.py:15
  15.3 7.6 %collective-permute-start.1 = (bf16[2,512,1,128]{1,3,2,0:T(8,128)(2,1)S(1)}, bf16[2,512,1,128]{1,3,2,0:T(8,128)(2,1)S(1)}, u32[]{:S(2)}, u32[]{:S(2)}) collective-permute-start(bf16[2,512,1,128]{1,3,2,0:T(8,128)(2,1)S(1)} %get-tuple-element.16), channel_id=1, source_target_pairs={{64,0},{128,64},{192,128},{0,192},{65,1},{129,65},{193,129},{1,193... | collective-permute-start | bytes 786440 | tf_op jit(solution)/shard_map/ppermute | solution.py:18
  29.7 14.6 %copy-start.10 = (s32[1,64]{1,0:T(1,128)S(1)}, s32[1,64]{1,0:T(1,128)}, u32[]{:S(2)}) copy-start(s32[1,64]{1,0:T(1,128)} %param.9) | copy-start | bytes 772
  29.7 54.9 %all-to-all-start = ((bf16[2,64,8,6,128]{4,2,3,0,1:T(8,128)(2,1)}), bf16[2,64,8,6,128]{4,2,3,0,1:T(8,128)(2,1)}, u32[]{:S(2)}, u32[]{:S(2)}) async-start(bf16[2,64,8,6,128]{4,2,3,0,1:T(8,128)(2,1)} %copy.438), calls=%async_computation | async-start | bytes 3145728 | tf_op jit(solution)/shard_map/all_to_all | solution.py:64
  191.7 2.2 copy-start.3
  191.8 4.9 %copy-start.7 = (bf16[64,2,1,8,6,128]{5,3,4,2,0,1:T(8,128)(2,1)}, bf16[64,2,1,8,6,128]{5,3,4,2,0,1:T(8,128)(2,1)S(1)}, u32[]{:S(2)}) copy-start(bf16[64,2,1,8,6,128]{5,3,4,2,0,1:T(8,128)(2,1)S(1)} %copy.721) | copy-start | bytes 4718596
  204.3 1.5 copy-start.4
  205.9 7.8 %collective-permute-start.2 = (bf16[2,512,1,128]{1,3,2,0:T(8,128)(2,1)S(1)}, bf16[2,512,1,128]{1,3,2,0:T(8,128)(2,1)S(1)}, u32[]{:S(2)}, u32[]{:S(2)}) collective-permute-start(bf16[2,512,1,128]{1,3,2,0:T(8,128)(2,1)S(1)} %get-tuple-element.9), channel_id=1, source_target_pairs={{0,64},{64,128},{128,192},{192,0},{1,65},{65,129},{129,193},{193,1... | collective-permute-start | bytes 786440 | tf_op jit(solution)/shard_map/ppermute | solution.py:15
  206.0 7.7 %collective-permute-start.3 = (bf16[2,512,1,128]{1,3,2,0:T(8,128)(2,1)S(1)}, bf16[2,512,1,128]{1,3,2,0:T(8,128)(2,1)S(1)}, u32[]{:S(2)}, u32[]{:S(2)}) collective-permute-start(bf16[2,512,1,128]{1,3,2,0:T(8,128)(2,1)S(1)} %get-tuple-element.10), channel_id=1, source_target_pairs={{64,0},{128,64},{192,128},{0,192},{65,1},{129,65},{193,129},{1,193... | collective-permute-start | bytes 786440 | tf_op jit(solution)/shard_map/ppermute | solution.py:18
  270.7 48.7 %copy-start.1 = (bf16[1,64,64]{2,1,0:T(8,128)(2,1)S(1)}, bf16[1,64,64]{2,1,0:T(8,128)(2,1)}, u32[]{:S(2)}) copy-start(bf16[1,64,64]{2,1,0:T(8,128)(2,1)} %param.8) | copy-start | bytes 24580
